TPU v7x, 512 devices: a whole 4x4x16 slice. The times are simulated.
512 devices in a mesh: layer: 16 (over y, x), dp: 32 (over z, core).
Axes of the slice: x: 4, y: 4, z: 16, core: 2. Of those that a mesh axis runs over, the one named last changes fastest.
Arguments:
- inputs: bfloat16 [4096, 1024], P('dp'), may hold values from -6 to 6
- guess_fwd: float32 [16, 4096, 1024], P('layer', 'dp'), may hold values from -9 to 9
- guess_adj: float32 [16, 4096, 1024], P('layer', 'dp'), may hold values from -6 to 6
- weights: bfloat16 [32, 1024, 1024], P('layer', 'dp'), may hold values from -0.1875 to 0.1875
- biases: float32 [32, 1024], P('layer'), may hold values from -3 to 3
- gains: float32 [16, 1024], P('layer'), may hold values from 0.6 to 1
- cotangent: bfloat16 [4096, 1024], P('dp'), may hold values from -6 to 6
Outputs:
- block_ends: float32 [16, 4096, 1024], P('layer', 'dp')
- block_adjoints: float32 [16, 4096, 1024], P('layer', 'dp')
- weight_grad: float32 [32, 1024, 1024], P('layer', 'dp')
- coarse_ends: float32 [16, 4096, 1024], P('layer', 'dp')
- coarse_adjoints: float32 [16, 4096, 1024], P('layer', 'dp')
All inputs are finite; a program needn't handle non-finite values.
Results may differ from a plain program's by a relative error of at most 0.024.
Values may be sent and summed in bfloat16 or wider, within the bound.
No kernel may reach another device: no remote copies, remote signals or barrier semaphores. Data moves between devices by JAX's collectives and lax.ppermute only.
A program may use at most 64 MiB of HBM per device.

v0:
```python
import jax
import jax.numpy as jnp
from jax import lax
from jax.sharding import PartitionSpec as P

step_size = 0.5


def from_behind(block, axis, distance):
    devices = range(lax.axis_size(axis))
    route = [(i - distance, i) for i in devices if i - distance in devices]
    return lax.ppermute(block, axis, route)


def prefix(shard, axis, combine, identity, reverse):
    size, place = (lax.axis_size(axis), lax.axis_index(axis))
    everything = jax.tree.map(lambda part: lax.all_gather(part, axis), shard)
    start = jax.tree.map(
        lambda part, zero: jnp.broadcast_to(jnp.asarray(zero, part.dtype), part.shape),
        shard,
        identity,
    )

    def hop(k, before):
        at = size - 1 - k if reverse else k
        reached = at > place if reverse else at < place
        new = combine(before, jax.tree.map(lambda part: part[at], everything))
        return jax.tree.map(lambda a, b: jnp.where(reached, a, b), new, before)

    return lax.fori_loop(0, size, hop, start)


def combine(earlier, later):
    return (earlier[0] * later[0], earlier[1] * later[0] + later[1])


def forward_block(start, weights, biases):
    state = start
    kept = []
    slopes = []
    for j in range(weights.shape[0]):
        rounded = state.astype(jnp.bfloat16)
        active = jnp.tanh(
            jnp.dot(rounded, weights[j], preferred_element_type=jnp.float32) + biases[j]
        )
        kept.append(rounded)
        slopes.append(1.0 - active * active)
        state = state + step_size * active
    return (state, kept, slopes)


def back_layer(adjoint, weight, slope):
    scaled = (adjoint * slope).astype(jnp.bfloat16)
    moved = lax.dot_general(
        scaled, weight, (((1,), (1,)), ((), ())), preferred_element_type=jnp.float32
    )
    return (adjoint + step_size * moved, scaled)


def backward_block(end, weights, slopes):
    adjoint = end
    for j in reversed(range(weights.shape[0])):
        adjoint = back_layer(adjoint, weights[j], slopes[j])[0]
    return adjoint


def grad_term(kept_rows, scaled):
    return step_size * lax.dot_general(
        kept_rows, scaled, (((0,), (0,)), ((), ())), preferred_element_type=jnp.float32
    )


def local(inputs, guess_fwd, guess_adj, weights, biases, gains, cotangent):
    full_weights = lax.all_gather(weights, "dp", axis=1, tiled=True)
    count = lax.axis_size("layer")
    index = lax.axis_index("layer")
    is_first = index == 0
    is_last = index == count - 1
    anchor = inputs.astype(jnp.float32)
    guess = guess_fwd[0]
    identity = (jnp.ones_like(gains), jnp.zeros_like(guess))
    arrived = from_behind(guess, "layer", 1)
    start = jnp.where(is_first, anchor, arrived)
    end_state = forward_block(start, full_weights, biases)[0]
    resid = end_state - guess
    factor, carried = prefix((gains, resid), "layer", combine, identity, False)
    guess = guess + (gains * carried + resid)
    start = jnp.where(is_first, anchor, from_behind(guess, "layer", 1))
    end_state, kept, slopes = forward_block(start, full_weights, biases)
    final_adj = cotangent.astype(jnp.float32)
    lam = guess_adj[0]
    arrived_adj = from_behind(lam, "layer", -1)
    end_adj = jnp.where(is_last, final_adj, arrived_adj)
    back = backward_block(end_adj, full_weights, slopes)
    resid_adj = back - lam
    factor_adj, carried_adj = prefix((gains, resid_adj), "layer", combine, identity, True)
    lam = lam + (gains * carried_adj + resid_adj)
    end_adj = jnp.where(is_last, final_adj, from_behind(lam, "layer", -1))
    adjoint = end_adj
    grads = [None] * full_weights.shape[0]
    for j in reversed(range(full_weights.shape[0])):
        adjoint, scaled = back_layer(adjoint, full_weights[j], slopes[j])
        grads[j] = lax.psum_scatter(
            grad_term(kept[j], scaled).astype(jnp.bfloat16), "dp", scatter_dimension=0, tiled=True
        ).astype(jnp.float32)
    return (end_state[None], adjoint[None], jnp.stack(grads), guess[None], lam[None])


def solution(mesh):
    return jax.shard_map(
        local,
        mesh=mesh,
        in_specs=(
            P("dp", None),
            P("layer", "dp", None),
            P("layer", "dp", None),
            P("layer", "dp", None),
            P("layer", None),
            P("layer", None),
            P("dp", None),
        ),
        out_specs=(
            P("layer", "dp", None),
            P("layer", "dp", None),
            P("layer", "dp", None),
            P("layer", "dp", None),
            P("layer", "dp", None),
        ),
        check_vma=False,
    )
```

profile of v0, /device:TPU:12, one launch (start us, length us, event | category | flops | bytes accessed | tf_op | source)
XLA Modules:
  0.0 589.8 jit_solution(7781073490397683310)
XLA Ops:
  7.2 0.7 all-gather.8.cloned.1.call-update
  8.0 3.1 collective-permute-start
  11.1 0.8 fusion.49
  11.9 11.9 %collective-permute-done = f32[128,1024]{1,0:T(8,128)S(1)} collective-permute-done((f32[128,1024]{1,0:T(8,128)}, f32[128,1024]{1,0:T(8,128)S(1)}, u32[]{:S(2)}, u32[]{:S(2)}) %collective-permute-start) | collective-permute-done | bytes 524320 | tf_op jit(solution)/shard_map/ppermute | solution.py:12
  23.7 64.3 %all-gather.8.cloned.1.call-done = bf16[2,1024,1024]{2,1,0:T(8,128)(2,1)} async-done(((bf16[2,32,1024]{2,1,0:T(8,128)(2,1)}), bf16[2,1024,1024]{2,1,0:T(8,128)(2,1)}) %all-gather.8.cloned.1.call-update) | async-done | bytes 4194320 | tf_op jit(solution)/shard_map/all_gather | solution.py:74
  88.0 2.1 fusion.24
  90.2 2.9 fusion.14
  93.2 22.2 %all-gather.3 = f32[16,1,1024]{2,1,0:T(1,128)S(1)} all-gather(f32[1,1,1024]{2,1,0:T(1,128)S(1)} %bitcast.110), channel_id=2, replica_groups=mesh['layer'=16,'dp'=32] {'layer'}, dimensions={0}, use_global_device_ids=true | all-gather | bytes 69632 | tf_op jit(solution)/shard_map/all_gather | solution.py:17
  115.3 59.6 %all-gather.10.cloned.1.call-done = f32[2048,1024]{1,0:T(8,128)} async-done(((f32[128,1024]{1,0:T(8,128)}), f32[2048,1024]{1,0:T(8,128)}) %all-gather.10.cloned.1.call-update) | async-done | bytes 8388624 | tf_op jit(solution)/shard_map/all_gather | solution.py:17
  175.0 24.4 %while.30 = (s32[]{:T(128)}, f32[128,1024]{1,0:T(8,128)S(1)}, s32[]{:T(128)}, f32[16,1,1024]{2,1,0:T(1,128)S(1)}, f32[16,128,1024]{2,1,0:T(8,128)}, /*index=5*/s32[]{:T(128)}, s32[]{:T(128)}) while((s32[]{:T(128)}, f32[128,1024]{1,0:T(8,128)S(1)}, s32[]{:T(128)}, f32[16,1,1024]{2,1,0:T(1,128)S(1)}, f32[16,128,1024]{2,1,0:T(8,128)}, ...), condition=%wide.region_1.2_spmd.clone, body=%wide.region_0.1_spmd.clone.sunk | while | flops 524292 | bytes 1585265 | solution.py:30
  175.0 1.6 fusion.54
  176.6 1.5 fusion.54
  178.1 1.5 fusion.54
  179.6 1.5 fusion.54
  181.1 1.5 fusion.54
  182.7 1.5 fusion.54
  184.2 1.5 fusion.54
  185.7 1.5 fusion.54
  187.2 1.5 fusion.54
  188.8 1.5 fusion.54
  190.3 1.5 fusion.54
  191.8 1.5 fusion.54
  193.3 1.5 fusion.54
  194.9 1.5 fusion.54
  196.4 1.5 fusion.54
  197.9 1.5 fusion.54
  199.4 0.1 add_add_fusion.1
  199.6 3.1 collective-permute-start.1
  202.7 2.8 collective-permute-start.2
  205.5 9.5 %collective-permute-done.1 = f32[128,1024]{1,0:T(8,128)S(1)} collective-permute-done((f32[128,1024]{1,0:T(8,128)S(1)}, f32[128,1024]{1,0:T(8,128)S(1)}, u32[]{:S(2)}, u32[]{:S(2)}) %collective-permute-start.1) | collective-permute-done | bytes 524320 | tf_op jit(solution)/shard_map/ppermute | solution.py:12
  215.0 2.1 multiply_add_fusion
  217.1 0.5 fusion.16
  217.6 1.2 collective-permute-done.2
  218.8 2.1 fusion.18
  220.9 1.7 fusion.29
  222.7 88.4 %all-gather.12.cloned.1.call-done = f32[2048,1024]{1,0:T(8,128)} async-done(((f32[128,1024]{1,0:T(8,128)}), f32[2048,1024]{1,0:T(8,128)}) %all-gather.12.cloned.1.call-update) | async-done | bytes 8388624 | tf_op jit(solution)/shard_map/all_gather | solution.py:17
  311.0 24.4 %while.31 = (s32[]{:T(128)}, f32[128,1024]{1,0:T(8,128)S(1)}, s32[]{:T(128)}, f32[16,1,1024]{2,1,0:T(1,128)S(1)}, f32[16,128,1024]{2,1,0:T(8,128)}, /*index=5*/s32[]{:T(128)}, s32[]{:T(128)}, s32[]{:T(128)}, s32[]{:T(128)}) while((s32[]{:T(128)}, f32[128,1024]{1,0:T(8,128)S(1)}, s32[]{:T(128)}, f32[16,1,1024]{2,1,0:T(1,128)S(1)}, ...), condition=%wide.region_3.4_spmd.clone, body=%wide.region_2.3_spmd.clone.sunk | while | flops 524296 | bytes 1585327 | solution.py:30
  311.1 1.5 fusion.55
  312.6 1.5 fusion.55
  314.1 1.5 fusion.55
  315.6 1.5 fusion.55
  317.2 1.5 fusion.55
  318.7 1.5 fusion.55
  320.2 1.5 fusion.55
  321.7 1.5 fusion.55
  323.3 1.5 fusion.55
  324.8 1.5 fusion.55
  326.3 1.5 fusion.55
  327.9 1.5 fusion.55
  329.4 1.5 fusion.55
  330.9 1.5 fusion.55
  332.5 1.5 fusion.55
  334.0 1.5 fusion.55
  335.6 0.8 copy-done.7
  336.4 2.6 collective-permute-start.3
  339.0 12.9 %collective-permute-done.3 = f32[128,1024]{1,0:T(8,128)S(1)} collective-permute-done((f32[128,1024]{1,0:T(8,128)S(1)}, f32[128,1024]{1,0:T(8,128)S(1)}, u32[]{:S(2)}, u32[]{:S(2)}) %collective-permute-start.3) | collective-permute-done | bytes 524320 | tf_op jit(solution)/shard_map/ppermute | solution.py:12
  351.9 3.0 multiply_convert_fusion
  355.0 2.4 fusion.20
  357.5 2.0 multiply_convert_fusion.1
  359.6 0.9 add_bitcast_fusion
  360.4 3.2 fusion.32
  363.6 106.2 %reduce-scatter.5.cloned.1.call-done = bf16[32,1024]{1,0:T(8,128)(2,1)} async-done(((bf16[1024,1024]{1,0:T(8,128)(2,1)}), bf16[32,1024]{1,0:T(8,128)(2,1)}) %reduce-scatter.5.cloned.1.call-update) | async-done | bytes 65552 | tf_op jit(solution)/shard_map/reduce_scatter | solution.py:103
  469.8 111.9 %reduce-scatter.3.cloned.1.call-done = bf16[32,1024]{1,0:T(8,128)(2,1)} async-done(((bf16[1024,1024]{1,0:T(8,128)(2,1)}), bf16[32,1024]{1,0:T(8,128)(2,1)}) %reduce-scatter.3.cloned.1.call-update) | async-done | bytes 65552 | tf_op jit(solution)/shard_map/reduce_scatter | solution.py:103
  581.7 1.6 maximum_convert_fusion
  (66 shorter events, 0.7 us)
Async XLA Ops:
  7.2 83.0 %copy-start.3 = (f32[1,128,1024]{2,1,0:T(8,128)S(1)}, f32[1,128,1024]{2,1,0:T(8,128)}, u32[]{:S(2)}) copy-start(f32[1,128,1024]{2,1,0:T(8,128)} %param.12) | copy-start | bytes 1572868
  7.2 86.0 %copy-start.10 = (f32[1,1024]{1,0:T(1,128)S(1)}, f32[1,1024]{1,0:T(1,128)}, u32[]{:S(2)}) copy-start(f32[1,1024]{1,0:T(1,128)} %param.16) | copy-start | bytes 12292
  7.2 80.8 %all-gather.8.cloned.1.call-start = ((), (), s32[]{:S(2)}) async-start(), calls=%async_computation.2 | async-start | bytes 4325376 | tf_op jit(solution)/shard_map/all_gather | solution.py:74
  7.9 167.1 %all-gather.10.cloned.1.call-start = ((), (), s32[]{:S(2)}) async-start(), calls=%async_computation.5 | async-start | bytes 8912896 | tf_op jit(solution)/shard_map/all_gather | solution.py:17
  8.0 15.8 %collective-permute-start = (f32[128,1024]{1,0:T(8,128)}, f32[128,1024]{1,0:T(8,128)S(1)}, u32[]{:S(2)}, u32[]{:S(2)}) collective-permute-start(f32[128,1024]{1,0:T(8,128)} %bitcast.100), channel_id=1, source_target_pairs={{0,32},{32,64},{64,96},{96,128},{128,160},{160,192},{192,224},{224... | collective-permute-start | bytes 1572872 | tf_op jit(solution)/shard_map/ppermute | solution.py:12
  93.1 106.3 %copy-start.1 = (f32[128,1024]{1,0:T(8,128)S(1)}, f32[128,1024]{1,0:T(8,128)}, u32[]{:S(2)}) copy-start(f32[128,1024]{1,0:T(8,128)} %fusion.14) | copy-start | bytes 1572868
  93.1 218.0 %all-gather.12.cloned.1.call-start = ((), (), s32[]{:S(2)}) async-start(), calls=%async_computation.6 | async-start | bytes 8912896 | tf_op jit(solution)/shard_map/all_gather | solution.py:17
  175.0 27.7 %copy-start.4 = (f32[1,128,1024]{2,1,0:T(8,128)S(1)}, f32[1,128,1024]{2,1,0:T(8,128)}, u32[]{:S(2)}) copy-start(f32[1,128,1024]{2,1,0:T(8,128)} %param.13) | copy-start | bytes 1572868
  175.0 40.0 %copy-start.5 = (bf16[128,1024]{1,0:T(8,128)(2,1)S(1)}, bf16[128,1024]{1,0:T(8,128)(2,1)}, u32[]{:S(2)}) copy-start(bf16[128,1024]{1,0:T(8,128)(2,1)} %param.11) | copy-start | bytes 786436
  199.5 18.0 %copy-start.6 = (f32[128,1024]{1,0:T(8,128)}, f32[128,1024]{1,0:T(8,128)S(1)}, u32[]{:S(2)}) copy-start(f32[128,1024]{1,0:T(8,128)S(1)} %add_add_fusion.1) | copy-start | bytes 1572868
  199.6 15.4 %collective-permute-start.1 = (f32[128,1024]{1,0:T(8,128)S(1)}, f32[128,1024]{1,0:T(8,128)S(1)}, u32[]{:S(2)}, u32[]{:S(2)}) collective-permute-start(f32[128,1024]{1,0:T(8,128)S(1)} %add_add_fusion.1), channel_id=1, source_target_pairs={{0,32},{32,64},{64,96},{96,128},{128,160},{160,192},{192,224},{224... | collective-permute-start | bytes 1572872 | tf_op jit(solution)/shard_map/ppermute | solution.py:12
  202.7 16.2 %collective-permute-start.2 = (f32[128,1024]{1,0:T(8,128)S(1)}, f32[128,1024]{1,0:T(8,128)}, u32[]{:S(2)}, u32[]{:S(2)}) collective-permute-start(f32[128,1024]{1,0:T(8,128)S(1)} %bitcast.101), channel_id=1, source_target_pairs={{32,0},{64,32},{96,64},{128,96},{160,128},{192,160},{224,192},{256... | collective-permute-start | bytes 1572872 | tf_op jit(solution)/shard_map/ppermute | solution.py:12
  205.4 11.7 %copy-start = (bf16[2,1024,1024]{2,1,0:T(8,128)(2,1)S(1)}, bf16[2,1024,1024]{2,1,0:T(8,128)(2,1)}, u32[]{:S(2)}) copy-start(bf16[2,1024,1024]{2,1,0:T(8,128)(2,1)} %all-gather.8.cloned.1.call-done) | copy-start | bytes 12582916
  205.4 13.4 %copy-start.8 = (bf16[128,1024]{1,0:T(8,128)(2,1)S(1)}, bf16[128,1024]{1,0:T(8,128)(2,1)}, u32[]{:S(2)}) copy-start(bf16[128,1024]{1,0:T(8,128)(2,1)} %param.17) | copy-start | bytes 786436
  222.6 112.9 %copy-start.2 = (f32[128,1024]{1,0:T(8,128)S(1)}, f32[128,1024]{1,0:T(8,128)}, u32[]{:S(2)}) copy-start(f32[128,1024]{1,0:T(8,128)} %fusion.29) | copy-start | bytes 1572868
  222.6 247.2 %reduce-scatter.5.cloned.1.call-start = ((), (), s32[]{:S(2)}) async-start(), calls=%async_computation.4 | async-start | bytes 2162688 | tf_op jit(solution)/shard_map/reduce_scatter | solution.py:103
  335.6 0.8 copy-start.7
  336.4 18.6 %copy-start.9 = (bf16[128,1024]{1,0:T(8,128)(2,1)S(1)}, bf16[128,1024]{1,0:T(8,128)(2,1)}, u32[]{:S(2)}) copy-start(bf16[128,1024]{1,0:T(8,128)(2,1)} %param.17) | copy-start | bytes 786436
  336.4 15.5 %collective-permute-start.3 = (f32[128,1024]{1,0:T(8,128)S(1)}, f32[128,1024]{1,0:T(8,128)S(1)}, u32[]{:S(2)}, u32[]{:S(2)}) collective-permute-start(f32[128,1024]{1,0:T(8,128)S(1)} %add_add_fusion), channel_id=1, source_target_pairs={{32,0},{64,32},{96,64},{128,96},{160,128},{192,160},{224,192},{256... | collective-permute-start | bytes 1572872 | tf_op jit(solution)/shard_map/ppermute | solution.py:12
  355.0 226.7 %reduce-scatter.3.cloned.1.call-start = ((), (), s32[]{:S(2)}) async-start(), calls=%async_computation.3 | async-start | bytes 2162688 | tf_op jit(solution)/shard_map/reduce_scatter | solution.py:103
Sparse Core Ops, SparseCore 0:
  10.1 77.8 all-gather.7
  93.2 81.7 all-gather.9
  222.7 88.2 all-gather.11
  355.1 114.6 reduce-scatter.4
  472.4 109.1 reduce-scatter.2
where the time goes:
time: 592 us; the launch traced here: 590 us
  waiting for transfers between devices  467 us (79%)
  other arithmetic  50.3 us (8%)
  blocking collectives  22.2 us (4%)
  matrix products  22 us (4%)
  between operations  14.1 us (2%)
  starting transfers between devices  11.7 us (2%)
    reduce_scatter x2, waiting for transfers between devices, local(): lax.psum_scatter(grad_term(kept[j], scaled).astype(jnp.bfloat16), 'dp', s...  218 us
    all_gather x2, waiting for transfers between devices, prefix(): everything = jax.tree.map(lambda part: lax.all_gather(part, axis), shard)  148 us
    all_gather x1, waiting for transfers between devices, local(): full_weights = lax.all_gather(weights, 'dp', axis=1, tiled=True)  64.3 us
    select_n x32, other arithmetic, hop(): return jax.tree.map(lambda a, b: jnp.where(reached, a, b), new, before)  47.6 us
    ppermute x4, waiting for transfers between devices, from_behind(): return lax.ppermute(block, axis, route)  35.5 us
    all_gather x1, blocking collectives, prefix(): everything = jax.tree.map(lambda part: lax.all_gather(part, axis), shard)  22.2 us
  transfers between devices with their start and end apart: 9, of which 9 were waited for; matrix products, arithmetic and copies ran while one was open for 2% of the time, Pallas kernels for 0%

commit v1 on v0

--- a/solution.py
+++ b/solution.py
@@ -71,7 +71,8 @@
 
 
 def local(inputs, guess_fwd, guess_adj, weights, biases, gains, cotangent):
-    full_weights = lax.all_gather(weights, "dp", axis=1, tiled=True)
+    repeated = jnp.stack([weights] * lax.axis_size("dp"))
+    full_weights = jnp.concatenate(lax.all_to_all(repeated, "dp", 0, 0), axis=1)
     count = lax.axis_size("layer")
     index = lax.axis_index("layer")
     is_first = index == 0

time: 592 us -> 720 us (1.22)
  the two profiles are of different devices: /device:TPU:12 before, /device:TPU:2 now
where the time goes in v1:
time: 720 us; the launch traced here: 717 us
  waiting for transfers between devices  570 us (79%)
  other arithmetic  53.4 us (7%)
  starting transfers between devices  27.6 us (4%)
  blocking collectives  23.7 us (3%)
  matrix products  17.1 us (2%)
  between operations  14.1 us (2%)
  local copies, waits for them, and re-layouts  10.3 us (1%)
    reduce_scatter x2, waiting for transfers between devices, local(): lax.psum_scatter(grad_term(kept[j], scaled).astype(jnp.bfloat16), 'dp', s...  216 us
    all_to_all x1, waiting for transfers between devices, local(): full_weights = jnp.concatenate(lax.all_to_all(repeated, 'dp', 0, 0), axis=1)  180 us
    all_gather x2, waiting for transfers between devices, prefix(): everything = jax.tree.map(lambda part: lax.all_gather(part, axis), shard)  151 us
    select_n x32, other arithmetic, hop(): return jax.tree.map(lambda a, b: jnp.where(reached, a, b), new, before)  47.6 us
    all_gather x1, blocking collectives, prefix(): everything = jax.tree.map(lambda part: lax.all_gather(part, axis), shard)  23.7 us
    ppermute x4, waiting for transfers between devices, from_behind(): return lax.ppermute(block, axis, route)  23.6 us
    all_to_all x1, starting transfers between devices, local(): full_weights = jnp.concatenate(lax.all_to_all(repeated, 'dp', 0, 0), axis=1)  15.7 us
  transfers between devices with their start and end apart: 9, of which 8 were waited for; matrix products, arithmetic and copies ran while one was open for 2% of the time, Pallas kernels for 0%

profile of v1, /device:TPU:2, one launch (start us, length us, event | category | flops | bytes accessed | tf_op | source)
XLA Modules:
  0.0 717.5 jit_solution(16984279918396398242)
XLA Ops:
  7.2 3.5 stack.13
  10.6 15.7 %all-to-all-start = ((bf16[32,2,32,1024]{3,2,1,0:T(8,128)(2,1)}), bf16[32,2,32,1024]{3,2,1,0:T(8,128)(2,1)}, u32[]{:S(2)}, u32[]{:S(2)}) async-start(bf16[32,2,32,1024]{3,2,1,0:T(8,128)(2,1)} %stack.13), calls=%async_computation | async-start | bytes 8388608 | tf_op jit(solution)/shard_map/all_to_all | solution.py:75
  26.4 3.4 collective-permute-start
  29.9 180.0 %all-to-all-done = bf16[32,2,32,1024]{3,2,1,0:T(8,128)(2,1)} async-done(((bf16[32,2,32,1024]{3,2,1,0:T(8,128)(2,1)}), bf16[32,2,32,1024]{3,2,1,0:T(8,128)(2,1)}, u32[]{:S(2)}, u32[]{:S(2)}) %all-to-all-start) | async-done | bytes 4194336 | tf_op jit(solution)/shard_map/all_to_all | solution.py:75
  209.9 2.9 fusion.33
  213.3 0.9 copy-done
  214.1 1.3 fusion.13
  215.5 23.7 %all-gather.3 = f32[16,1,1024]{2,1,0:T(1,128)S(1)} all-gather(f32[1,1,1024]{2,1,0:T(1,128)S(1)} %bitcast.67), channel_id=2, replica_groups=mesh['layer'=16,'dp'=32] {'layer'}, dimensions={0}, use_global_device_ids=true | all-gather | bytes 69632 | tf_op jit(solution)/shard_map/all_gather | solution.py:17
  239.2 61.5 %all-gather.7.cloned.1.call-done = f32[2048,1024]{1,0:T(8,128)} async-done(((f32[128,1024]{1,0:T(8,128)}), f32[2048,1024]{1,0:T(8,128)}) %all-gather.7.cloned.1.call-update) | async-done | bytes 8388624 | tf_op jit(solution)/shard_map/all_gather | solution.py:17
  300.8 24.4 %while.30 = (s32[]{:T(128)}, f32[128,1024]{1,0:T(8,128)S(1)}, s32[]{:T(128)}, f32[16,1,1024]{2,1,0:T(1,128)S(1)}, f32[16,128,1024]{2,1,0:T(8,128)}, /*index=5*/s32[]{:T(128)}, s32[]{:T(128)}) while((s32[]{:T(128)}, f32[128,1024]{1,0:T(8,128)S(1)}, s32[]{:T(128)}, f32[16,1,1024]{2,1,0:T(1,128)S(1)}, f32[16,128,1024]{2,1,0:T(8,128)}, ...), condition=%wide.region_1.2_spmd.clone, body=%wide.region_0.1_spmd.clone.sunk | while | flops 524292 | bytes 1585265 | solution.py:30
  300.8 1.5 fusion.47
  302.3 1.5 fusion.47
  303.9 1.5 fusion.47
  305.4 1.5 fusion.47
  306.9 1.5 fusion.47
  308.4 1.5 fusion.47
  310.0 1.5 fusion.47
  311.5 1.5 fusion.47
  313.0 1.5 fusion.47
  314.5 1.5 fusion.47
  316.0 1.5 fusion.47
  317.6 1.5 fusion.47
  319.1 1.5 fusion.47
  320.6 1.5 fusion.47
  322.1 1.5 fusion.47
  323.7 1.5 fusion.47
  325.2 2.0 add_add_fusion.1
  327.1 3.4 collective-permute-start.1
  330.5 2.5 collective-permute-start.2
  333.0 9.7 %collective-permute-done.1 = f32[128,1024]{1,0:T(8,128)S(1)} collective-permute-done((f32[128,1024]{1,0:T(8,128)}, f32[128,1024]{1,0:T(8,128)S(1)}, u32[]{:S(2)}, u32[]{:S(2)}) %collective-permute-start.1) | collective-permute-done | bytes 524320 | tf_op jit(solution)/shard_map/ppermute | solution.py:12
  343.5 0.8 copy-done.2
  345.0 0.9 collective-permute-done.2
  345.9 2.1 fusion.7
  348.0 2.7 fusion.6
  350.8 89.0 %all-gather.9.cloned.1.call-done = f32[2048,1024]{1,0:T(8,128)} async-done(((f32[128,1024]{1,0:T(8,128)}), f32[2048,1024]{1,0:T(8,128)}) %all-gather.9.cloned.1.call-update) | async-done | bytes 8388624 | tf_op jit(solution)/shard_map/all_gather | solution.py:17
  439.8 24.4 %while.31 = (s32[]{:T(128)}, f32[128,1024]{1,0:T(8,128)S(1)}, s32[]{:T(128)}, f32[16,1,1024]{2,1,0:T(1,128)S(1)}, f32[16,128,1024]{2,1,0:T(8,128)}, /*index=5*/s32[]{:T(128)}, s32[]{:T(128)}, s32[]{:T(128)}, s32[]{:T(128)}) while((s32[]{:T(128)}, f32[128,1024]{1,0:T(8,128)S(1)}, s32[]{:T(128)}, f32[16,1,1024]{2,1,0:T(1,128)S(1)}, ...), condition=%wide.region_3.4_spmd.clone, body=%wide.region_2.3_spmd.clone.sunk | while | flops 524296 | bytes 1585327 | solution.py:30
  439.8 1.5 fusion.48
  441.3 1.5 fusion.48
  442.9 1.5 fusion.48
  444.4 1.5 fusion.48
  445.9 1.5 fusion.48
  447.4 1.5 fusion.48
  449.0 1.5 fusion.48
  450.5 1.5 fusion.48
  452.0 1.5 fusion.48
  453.6 1.5 fusion.48
  455.1 1.5 fusion.48
  456.6 1.5 fusion.48
  458.1 1.5 fusion.48
  459.7 1.5 fusion.48
  461.2 1.5 fusion.48
  462.7 1.5 fusion.48
  464.2 1.4 add_add_fusion
  466.4 2.5 collective-permute-start.3
  468.9 12.9 %collective-permute-done.3 = f32[128,1024]{1,0:T(8,128)S(1)} collective-permute-done((f32[128,1024]{1,0:T(8,128)S(1)}, f32[128,1024]{1,0:T(8,128)S(1)}, u32[]{:S(2)}, u32[]{:S(2)}) %collective-permute-start.3) | collective-permute-done | bytes 524320 | tf_op jit(solution)/shard_map/ppermute | solution.py:12
  481.8 2.1 multiply_convert_fusion
  484.0 2.5 fusion.4
  486.5 0.8 copy-done.7
  487.3 2.1 multiply_convert_fusion.1
  489.4 0.9 add_bitcast_fusion
  490.3 3.0 fusion.3
  493.3 104.2 %reduce-scatter.5.cloned.1.call-done = bf16[32,1024]{1,0:T(8,128)(2,1)} async-done(((bf16[1024,1024]{1,0:T(8,128)(2,1)}), bf16[32,1024]{1,0:T(8,128)(2,1)}) %reduce-scatter.5.cloned.1.call-update) | async-done | bytes 65552 | tf_op jit(solution)/shard_map/reduce_scatter | solution.py:104
  597.5 111.9 %reduce-scatter.3.cloned.1.call-done = bf16[32,1024]{1,0:T(8,128)(2,1)} async-done(((bf16[1024,1024]{1,0:T(8,128)(2,1)}), bf16[32,1024]{1,0:T(8,128)(2,1)}) %reduce-scatter.3.cloned.1.call-update) | async-done | bytes 65552 | tf_op jit(solution)/shard_map/reduce_scatter | solution.py:104
  709.4 1.6 maximum_convert_fusion
  (79 shorter events, 3.2 us)
Async XLA Ops:
  10.6 15.8 %copy-start.13 = (f32[1,128,1024]{2,1,0:T(8,128)S(1)}, f32[1,128,1024]{2,1,0:T(8,128)}, u32[]{:S(2)}) copy-start(f32[1,128,1024]{2,1,0:T(8,128)} %param.12) | copy-start | bytes 1572868
  10.6 19.2 %copy-start.16 = (f32[2,1024]{1,0:T(2,128)S(1)}, f32[2,1024]{1,0:T(2,128)}, u32[]{:S(2)}) copy-start(f32[2,1024]{1,0:T(2,128)} %param.15) | copy-start | bytes 24580
  10.6 199.3 %all-to-all-start = ((bf16[32,2,32,1024]{3,2,1,0:T(8,128)(2,1)}), bf16[32,2,32,1024]{3,2,1,0:T(8,128)(2,1)}, u32[]{:S(2)}, u32[]{:S(2)}) async-start(bf16[32,2,32,1024]{3,2,1,0:T(8,128)(2,1)} %stack.13), calls=%async_computation | async-start | bytes 8388608 | tf_op jit(solution)/shard_map/all_to_all | solution.py:75
  26.4 274.4 %all-gather.7.cloned.1.call-start = ((), (), s32[]{:S(2)}) async-start(), calls=%async_computation.5 | async-start | bytes 8912896 | tf_op jit(solution)/shard_map/all_gather | solution.py:17
  26.4 186.3 %collective-permute-start = (f32[128,1024]{1,0:T(8,128)S(1)}, f32[128,1024]{1,0:T(8,128)S(1)}, u32[]{:S(2)}, u32[]{:S(2)}) collective-permute-start(f32[128,1024]{1,0:T(8,128)S(1)} %bitcast.59), channel_id=1, source_target_pairs={{0,32},{32,64},{64,96},{96,128},{128,160},{160,192},{192,224},{224... | collective-permute-start | bytes 1572872 | tf_op jit(solution)/shard_map/ppermute | solution.py:12
  209.9 2.9 copy-start.10
  212.8 1.4 copy-start
  214.1 1.4 copy-start.15
  215.4 224.4 %all-gather.9.cloned.1.call-start = ((), (), s32[]{:S(2)}) async-start(), calls=%async_computation.6 | async-start | bytes 8912896 | tf_op jit(solution)/shard_map/all_gather | solution.py:17
  300.8 24.4 %copy-start.8 = (f32[128,1024]{1,0:T(8,128)S(1)}, f32[128,1024]{1,0:T(8,128)}, u32[]{:S(2)}) copy-start(f32[128,1024]{1,0:T(8,128)} %fusion.13) | copy-start | bytes 1572868
  327.1 15.6 %collective-permute-start.1 = (f32[128,1024]{1,0:T(8,128)}, f32[128,1024]{1,0:T(8,128)S(1)}, u32[]{:S(2)}, u32[]{:S(2)}) collective-permute-start(f32[128,1024]{1,0:T(8,128)} %add_add_fusion.1), channel_id=1, source_target_pairs={{0,32},{32,64},{64,96},{96,128},{128,160},{160,192},{192,224},{224... | collective-permute-start | bytes 1572872 | tf_op jit(solution)/shard_map/ppermute | solution.py:12
  330.5 15.4 %collective-permute-start.2 = (f32[128,1024]{1,0:T(8,128)}, f32[128,1024]{1,0:T(8,128)}, u32[]{:S(2)}, u32[]{:S(2)}) collective-permute-start(f32[128,1024]{1,0:T(8,128)} %bitcast.10), channel_id=1, source_target_pairs={{32,0},{64,32},{96,64},{128,96},{160,128},{192,160},{224,192},{256... | collective-permute-start | bytes 1572872 | tf_op jit(solution)/shard_map/ppermute | solution.py:12
  342.8 0.7 copy-start.11
  342.8 1.7 copy-start.1
  343.5 0.8 copy-start.2
  343.5 4.5 copy-start.5
  343.5 2.4 copy-start.9
  350.7 246.8 %reduce-scatter.5.cloned.1.call-start = ((), (), s32[]{:S(2)}) async-start(), calls=%async_computation.4 | async-start | bytes 2162688 | tf_op jit(solution)/shard_map/reduce_scatter | solution.py:104
  464.2 17.6 %copy-start.3 = (f32[128,1024]{1,0:T(8,128)S(1)}, f32[128,1024]{1,0:T(8,128)}, u32[]{:S(2)}) copy-start(f32[128,1024]{1,0:T(8,128)} %copy-done.2) | copy-start | bytes 1572868
  465.6 0.8 copy-start.14
  466.4 15.4 %collective-permute-start.3 = (f32[128,1024]{1,0:T(8,128)S(1)}, f32[128,1024]{1,0:T(8,128)S(1)}, u32[]{:S(2)}, u32[]{:S(2)}) collective-permute-start(f32[128,1024]{1,0:T(8,128)S(1)} %add_add_fusion), channel_id=1, source_target_pairs={{32,0},{64,32},{96,64},{128,96},{160,128},{192,160},{224,192},{256... | collective-permute-start | bytes 1572872 | tf_op jit(solution)/shard_map/ppermute | solution.py:12
  483.9 225.4 %reduce-scatter.3.cloned.1.call-start = ((), (), s32[]{:S(2)}) async-start(), calls=%async_computation.3 | async-start | bytes 2162688 | tf_op jit(solution)/shard_map/reduce_scatter | solution.py:104
  484.0 3.4 copy-start.6
  484.0 3.3 copy-start.12
  486.5 0.8 copy-start.7
  487.3 2.1 copy-start.4
Sparse Core Ops, SparseCore 0:
  215.5 85.1 all-gather.6
  350.8 88.9 all-gather.8
  484.1 113.3 reduce-scatter.4
  600.1 109.1 reduce-scatter.2
